TPU v7x, 32 devices: a whole 2x2x4 slice. The times are simulated.
32 devices in a mesh: section: 2 (over y), dp: 4 (over z), tensor: 4 (over x, core).
Axes of the slice: x: 2, y: 2, z: 4, core: 2. Of those that a mesh axis runs over, the one named last changes fastest.
Arguments:
- tokens: bfloat16 [2048, 1088], P(('dp', 'tensor')), may hold values from -6 to 6
- lengths: int32 [16, 2, 4], P(('dp', 'tensor')), may hold values from 1 to 42, 64 in all within a row
- w_qkv: bfloat16 [2, 1088, 3264], P('section'), may hold values from -2 to 2, as said below
- w_out: bfloat16 [2, 1088, 1088], P('section'), may hold values from -0.375 to 0.375
- w_up: bfloat16 [2, 1088, 4352], P('section', None, 'tensor'), may hold values from -0.1875 to 0.1875
- up_bias: float32 [2, 4352], P('section', 'tensor'), may hold values from -3 to 3
- w_down: bfloat16 [2, 4352, 1088], P('section', 'tensor'), may hold values from -0.09375 to 0.09375
- gains: float32 [2, 2, 1088], P('section'), may hold values from 0.25 to 1.75
- biases: float32 [2, 6, 1088], P('section'), may hold values from -2.5 to 2.5
- cotangent: bfloat16 [2048, 1088], P(('dp', 'tensor')), may hold values from -6 to 6
Outputs:
- layer_outputs: bfloat16 [2, 2048, 1088], P('section', ('dp', 'tensor'))
- input_grads: bfloat16 [2, 2048, 1088], P('section', ('dp', 'tensor'))
- grad_w_qkv: float32 [2, 1088, 3264], P('section', ('dp', 'tensor'))
- grad_w_out: float32 [2, 1088, 1088], P('section', ('dp', 'tensor'))
- grad_gains: float32 [2, 2, 1088], P('section', None, ('dp', 'tensor'))
- grad_biases: float32 [2, 6, 1088], P('section', None, ('dp', 'tensor'))
- grad_w_up: float32 [2, 1088, 4352], P('section', None, 'tensor')
- grad_up_bias: float32 [2, 4352], P('section', 'tensor')
- grad_w_down: float32 [2, 4352, 1088], P('section', 'tensor')
Inputs may be any that keep to these rules, and one draw needn't show every extreme that they name: Each device's rows of one micro-batch hold 4 whole sequences whose lengths sum to 64; the longest is 42. `w_qkv`: columns are queries, keys and values in that order.
All inputs are finite; a program needn't handle non-finite values.
Results may differ from a plain program's by a relative error of at most 0.025.
Values may be sent and summed in bfloat16 or wider, within the bound.
A program may use at most 192 MiB of HBM per device.

v0:
```python
import math

import jax
import jax.numpy as jnp
from jax import lax
from jax.sharding import PartitionSpec as P

HEADS = 17
ROWS_MB = 64
MICRO = 2


EPSILON = 1e-05
GELU_SCALE = math.sqrt(2.0 / math.pi)
GELU_CUBIC = 0.044715


def shifted(block, axis, distance):
    devices = range(lax.axis_size(axis))
    route = [(i - distance, i) for i in devices if i - distance in devices]
    return lax.ppermute(block, axis, route)


def norm_rows(values):
    centre = values - jnp.mean(values, axis=-1, keepdims=True)
    inverse = lax.rsqrt(jnp.mean(centre * centre, axis=-1, keepdims=True) + EPSILON)
    return (centre * inverse, inverse)


def norm_back(grad_normed, normed, inverse, gain):
    scaled = grad_normed * gain
    return (
        scaled
        - jnp.mean(scaled, axis=-1, keepdims=True)
        - normed * jnp.mean(scaled * normed, axis=-1, keepdims=True)
    ) * inverse


def gelu_tanh(values):
    return (
        0.5
        * values
        * (1.0 + jnp.tanh(GELU_SCALE * (values + GELU_CUBIC * values * values * values)))
    )


def gelu_slope(values):
    tangent = jnp.tanh(GELU_SCALE * (values + GELU_CUBIC * values * values * values))
    return 0.5 * (1.0 + tangent) + 0.5 * values * (1.0 - tangent * tangent) * GELU_SCALE * (
        1.0 + 3.0 * GELU_CUBIC * values * values
    )


def contract_rows(left, right):
    return lax.dot_general(
        left, right, (((0,), (0,)), ((), ())), preferred_element_type=jnp.float32
    )


def contract_cols(left, right):
    return lax.dot_general(
        left, right, (((1,), (1,)), ((), ())), preferred_element_type=jnp.float32
    )


def make_allowed(seq_lengths, row_count):
    ends = jnp.cumsum(seq_lengths)
    places = jnp.arange(row_count, dtype=jnp.int32)
    segment = jnp.sum((places[:, None] >= ends[None, :]).astype(jnp.int32), axis=1)
    return (segment[:, None] == segment[None, :]) & (places[None, :] <= places[:, None])


def head_split(values):
    return values.reshape(values.shape[0], HEADS, values.shape[1] // HEADS)


def masked_scores(queries, keys_all, allowed):
    head_width = queries.shape[1] // HEADS
    scores = jnp.einsum(
        "qhd,khd->hqk",
        head_split(queries),
        head_split(keys_all),
        preferred_element_type=jnp.float32,
    ) * head_width ** (-0.5)
    return jnp.where(allowed[None], scores, -jnp.inf)


def layer_forward(layer_in, allowed, params):
    w_qkv, w_out, w_up, up_bias, w_down, gains, biases = params
    row_count, model_width = layer_in.shape
    inflow = layer_in.astype(jnp.float32)
    normed_one, inverse_one = norm_rows(inflow)
    normal_one = (normed_one * gains[0] + biases[0]).astype(jnp.bfloat16)
    projected = jnp.dot(normal_one, w_qkv, preferred_element_type=jnp.float32)
    queries = (projected[:, :model_width] + biases[1]).astype(jnp.bfloat16)
    keys_all = projected[:, model_width : 2 * model_width].astype(jnp.bfloat16)
    values_all = (projected[:, 2 * model_width :] + biases[2]).astype(jnp.bfloat16)
    masked = masked_scores(queries, keys_all, allowed)
    peak = jnp.max(masked, axis=-1, keepdims=True)
    log_total = peak + jnp.log(jnp.sum(jnp.exp(masked - peak), axis=-1, keepdims=True))
    probs = jnp.exp(masked - log_total).astype(jnp.bfloat16)
    mixed = jnp.einsum(
        "hqk,khd->qhd", probs, head_split(values_all), preferred_element_type=jnp.float32
    )
    mixed = mixed.reshape(row_count, model_width).astype(jnp.bfloat16)
    residual = inflow + jnp.dot(mixed, w_out, preferred_element_type=jnp.float32) + biases[3]
    normed_two, inverse_two = norm_rows(residual)
    normal_two = (normed_two * gains[1] + biases[4]).astype(jnp.bfloat16)
    gathered = lax.all_gather(normal_two, "tensor", axis=0, tiled=True)
    hidden_pre = jnp.dot(gathered, w_up, preferred_element_type=jnp.float32) + up_bias
    hidden = gelu_tanh(hidden_pre).astype(jnp.bfloat16)
    branch = lax.psum_scatter(
        jnp.dot(hidden, w_down, preferred_element_type=jnp.float32).astype(jnp.bfloat16),
        "tensor",
        scatter_dimension=0,
        tiled=True,
    ).astype(jnp.float32)
    result = (residual + branch + biases[5]).astype(jnp.bfloat16)
    kept = (
        normal_one,
        normed_one,
        inverse_one,
        queries,
        keys_all,
        values_all,
        mixed,
        log_total,
        normed_two,
        inverse_two,
        gathered,
        hidden_pre,
        hidden,
    )
    return (result, kept)


def layer_backward(grad_out, kept, allowed, params):
    w_qkv, w_out, w_up, up_bias, w_down, gains, biases = params
    (
        normal_one,
        normed_one,
        inverse_one,
        queries,
        keys_all,
        values_all,
        mixed,
        log_total,
        normed_two,
        inverse_two,
        gathered,
        hidden_pre,
        hidden,
    ) = kept
    row_count, model_width = grad_out.shape
    head_width = model_width // HEADS
    grad_flow = grad_out.astype(jnp.float32)
    grad_rows = lax.all_gather(grad_out, "tensor", axis=0, tiled=True)
    grad_down = contract_rows(hidden, grad_rows)
    grad_hidden = contract_cols(grad_rows, w_down)
    grad_pre = grad_hidden * gelu_slope(hidden_pre)
    grad_up_bias = jnp.sum(grad_pre, axis=0)
    grad_pre_b = grad_pre.astype(jnp.bfloat16)
    grad_up = contract_rows(gathered, grad_pre_b)
    grad_two = lax.psum_scatter(
        contract_cols(grad_pre_b, w_up).astype(jnp.bfloat16),
        "tensor",
        scatter_dimension=0,
        tiled=True,
    ).astype(jnp.float32)
    grad_resid = grad_flow + norm_back(grad_two, normed_two, inverse_two, gains[1])
    grad_resid_b = grad_resid.astype(jnp.bfloat16)
    grad_wout = contract_rows(mixed, grad_resid_b)
    grad_mixed = contract_cols(grad_resid_b, w_out).astype(jnp.bfloat16)
    masked = masked_scores(queries, keys_all, allowed)
    probs_f = jnp.exp(masked - log_total)
    probs_b = probs_f.astype(jnp.bfloat16)
    grad_heads = head_split(grad_mixed)
    grad_probs = jnp.einsum(
        "qhd,khd->hqk", grad_heads, head_split(values_all), preferred_element_type=jnp.float32
    )
    grad_values = jnp.einsum(
        "hqk,qhd->khd", probs_b, grad_heads, preferred_element_type=jnp.float32
    ).reshape(row_count, model_width)
    centre = jnp.sum(probs_f * grad_probs, axis=-1, keepdims=True)
    grad_scores = (probs_f * (grad_probs - centre) * head_width ** (-0.5)).astype(jnp.bfloat16)
    grad_queries = jnp.einsum(
        "hqk,khd->qhd", grad_scores, head_split(keys_all), preferred_element_type=jnp.float32
    ).reshape(row_count, model_width)
    grad_keys = jnp.einsum(
        "hqk,qhd->khd", grad_scores, head_split(queries), preferred_element_type=jnp.float32
    ).reshape(row_count, model_width)
    grad_proj = jnp.concatenate([grad_queries, grad_keys, grad_values], axis=1).astype(jnp.bfloat16)
    grad_wqkv = contract_rows(normal_one, grad_proj)
    grad_one = contract_cols(grad_proj, w_qkv)
    grad_in = (grad_resid + norm_back(grad_one, normed_one, inverse_one, gains[0])).astype(
        jnp.bfloat16
    )
    gain_grads = jnp.stack(
        [jnp.sum(normed_one * grad_one, axis=0), jnp.sum(normed_two * grad_two, axis=0)]
    )
    bias_grads = jnp.stack(
        [
            jnp.sum(grad_one, axis=0),
            jnp.sum(grad_queries, axis=0),
            jnp.sum(grad_values, axis=0),
            jnp.sum(grad_resid, axis=0),
            jnp.sum(grad_two, axis=0),
            jnp.sum(grad_flow, axis=0),
        ]
    )
    return (
        grad_in,
        (grad_wqkv, grad_wout, gain_grads, bias_grads),
        (grad_up, grad_down, grad_up_bias),
    )


def per_device(tokens, lengths, w_qkv, w_out, w_up, up_bias, w_down, gains, biases, cotangent):
    section_index = lax.axis_index("section")
    model_width = tokens.shape[1]
    row_count = ROWS_MB
    micro_count = MICRO
    slot_count = micro_count + 1
    params = (w_qkv[0], w_out[0], w_up[0], up_bias[0], w_down[0], gains[0], biases[0])
    blank = jnp.zeros((row_count, model_width), jnp.bfloat16)
    inputs = jnp.concatenate(
        [tokens.reshape(micro_count, row_count, model_width), blank[None]], axis=0
    )
    cots = jnp.concatenate(
        [cotangent.reshape(micro_count, row_count, model_width), blank[None]], axis=0
    )
    seq_table = jnp.concatenate([lengths[0], lengths[0][:1]], axis=0)
    outputs_buf = jnp.zeros((slot_count, row_count, model_width), jnp.bfloat16)
    grads_buf = jnp.zeros((slot_count, row_count, model_width), jnp.bfloat16)
    arrived = blank
    store = None
    for step_index in range(slot_count):
        slot_index = jnp.mod(step_index - section_index, slot_count)
        own_rows = lax.dynamic_index_in_dim(inputs, slot_index, 0, keepdims=False)
        layer_in = jnp.where(section_index == 0, own_rows, arrived)
        allowed = make_allowed(
            lax.dynamic_index_in_dim(seq_table, slot_index, 0, keepdims=False), row_count
        )
        result, kept = layer_forward(layer_in, allowed, params)
        if store is None:
            store = jax.tree.map(
                lambda sample: jnp.zeros((slot_count,) + sample.shape, sample.dtype), kept
            )
        store = jax.tree.map(
            lambda whole_buf, new_part: lax.dynamic_update_index_in_dim(
                whole_buf, new_part, slot_index, 0
            ),
            store,
            kept,
        )
        outputs_buf = lax.dynamic_update_index_in_dim(outputs_buf, result, slot_index, 0)
        if step_index < micro_count:
            arrived = shifted(result, "section", 1)
    grad_arrived = blank
    shared_acc = None
    sharded_acc = None
    for step_index in range(slot_count):
        slot_index = jnp.mod(step_index - 1 + section_index, slot_count)
        is_live = slot_index < micro_count
        own_cot = lax.dynamic_index_in_dim(cots, slot_index, 0, keepdims=False)
        grad_out = jnp.where(section_index == 1, own_cot, grad_arrived)
        allowed = make_allowed(
            lax.dynamic_index_in_dim(seq_table, slot_index, 0, keepdims=False), row_count
        )
        kept_now = jax.tree.map(
            lambda whole_buf: lax.dynamic_index_in_dim(whole_buf, slot_index, 0, keepdims=False),
            store,
        )
        grad_in, shared, sharded = layer_backward(grad_out, kept_now, allowed, params)
        shared = jax.tree.map(lambda part_grad: jnp.where(is_live, part_grad, 0.0), shared)
        sharded = jax.tree.map(lambda part_grad: jnp.where(is_live, part_grad, 0.0), sharded)
        if shared_acc is None:
            shared_acc = tuple(shared)
            sharded_acc = tuple(sharded)
        else:
            shared_acc = tuple(jax.tree.map(jnp.add, tuple(shared_acc), tuple(shared)))
            sharded_acc = tuple(jax.tree.map(jnp.add, tuple(sharded_acc), tuple(sharded)))
        grads_buf = lax.dynamic_update_index_in_dim(grads_buf, grad_in, slot_index, 0)
        if step_index < micro_count:
            grad_arrived = shifted(grad_in, "section", -1)
    shared_acc = (
        lax.psum_scatter(shared_acc[0], ("dp", "tensor"), scatter_dimension=0, tiled=True),
        lax.psum_scatter(shared_acc[1], ("dp", "tensor"), scatter_dimension=0, tiled=True),
        lax.psum_scatter(shared_acc[2], ("dp", "tensor"), scatter_dimension=1, tiled=True),
        lax.psum_scatter(shared_acc[3], ("dp", "tensor"), scatter_dimension=1, tiled=True),
    )
    sharded_acc = (
        lax.psum(sharded_acc[0].astype(jnp.bfloat16), "dp").astype(jnp.float32),
        lax.psum(sharded_acc[1].astype(jnp.bfloat16), "dp").astype(jnp.float32),
        lax.psum(sharded_acc[2].astype(jnp.bfloat16), "dp").astype(jnp.float32),
    )
    layer_outputs = outputs_buf[:micro_count].reshape(1, micro_count * row_count, model_width)
    input_grads = grads_buf[:micro_count].reshape(1, micro_count * row_count, model_width)
    return (
        layer_outputs,
        input_grads,
        shared_acc[0][None],
        shared_acc[1][None],
        shared_acc[2][None],
        shared_acc[3][None],
        sharded_acc[0][None],
        sharded_acc[2][None],
        sharded_acc[1][None],
    )


def solution(mesh):
    in_specs = (
        P(("dp", "tensor"), None),
        P(("dp", "tensor"), None, None),
        P("section", None, None),
        P("section", None, None),
        P("section", None, "tensor"),
        P("section", "tensor"),
        P("section", "tensor", None),
        P("section", None, None),
        P("section", None, None),
        P(("dp", "tensor"), None),
    )
    out_specs = (
        P("section", ("dp", "tensor"), None),
        P("section", ("dp", "tensor"), None),
        P("section", ("dp", "tensor"), None),
        P("section", ("dp", "tensor"), None),
        P("section", None, ("dp", "tensor")),
        P("section", None, ("dp", "tensor")),
        P("section", None, "tensor"),
        P("section", "tensor"),
        P("section", "tensor", None),
    )
    return jax.shard_map(
        per_device, mesh=mesh, in_specs=in_specs, out_specs=out_specs, check_vma=False
    )
```

profile of v0, /device:TPU:0, one launch (start us, length us, event | category | flops | bytes accessed | tf_op | source)
XLA Modules:
  0.0 814.9 jit_solution(7323134262417438477)
XLA Ops:
  28.4 9.4 %all_gather.18 = bf16[256,1088]{1,0:T(8,128)(2,1)} all-gather(bf16[64,1088]{1,0:T(8,128)(2,1)S(1)} %add_convert_fusion.5), channel_id=1, replica_groups=mesh['section'=2,'dp'=4,'tensor'=4] {'tensor'}, dimensions={0}, use_global_device_ids=true | all-gather | bytes 696320 | tf_op jit(solution)/shard_map/all_gather | solution.py:109
  79.5 8.1 all-gather
  114.3 7.1 all_gather.19
  146.0 12.7 %reduce-scatter.15.cloned.1.call-done = bf16[64,1088]{1,0:T(8,128)(2,1)} async-done(((bf16[256,1088]{1,0:T(8,128)(2,1)}), bf16[64,1088]{1,0:T(8,128)(2,1)}) %reduce-scatter.15.cloned.1.call-update) | async-done | bytes 139280 | tf_op jit(solution)/shard_map/reduce_scatter | solution.py:112
  178.9 7.2 all_gather.20
  226.9 4.5 convolution_select_fusion.5
  234.9 7.9 reduce-scatter.19.cloned.1.call-done
  264.4 6.3 fusion.235
  281.5 6.9 all_gather.22
  343.3 5.7 fusion.229
  361.0 7.3 all_gather.23
  374.8 4.5 convolution_select_fusion.3
  379.4 12.2 %psum.22 = bf16[1,1088]{1,0:T(2,128)(2,1)S(1)} all-reduce(bf16[1,1088]{1,0:T(2,128)(2,1)S(1)} %broadcast_in_dim.354), channel_id=1, replica_groups=mesh['section'=2,'dp'=4,'tensor'=4] {'dp'}, use_global_device_ids=true, to_apply=%region_83.84 | all-reduce | flops 1088 | bytes 4352 | tf_op jit(solution)/shard_map/psum | solution.py:295
  392.2 5.1 fusion.27
  397.3 5.2 fusion.28
  416.1 5.4 fusion.15
  425.6 8.2 %convolution_select_fusion.1 = f32[1088,3264]{1,0:T(8,128)} fusion(pred[]{:T(512)S(6)} %lt.169, bf16[64,1088]{0,1:T(8,128)(2,1)S(1)} %bitcast.554, bf16[64,1088]{0,1:T(8,128)(2,1)S(1)} %bitcast.596, bf16[64,1088]{0,1:T(8,128)(2,1)S(1)} %bitcast.552, bf16[3,64,1088]{1,2,0:T(8,128)(2,1)} %constant_dynamic-update-slice_fusion.6, s32[]{:T(128)S(6)} %select_n.354), kind=kOutput, calls=%fused_computation.4 | convolution fusion | flops 459362304 | bytes 14901253 | tf_op jit(solution)/shard_map/dot_general | solution.py:55
  433.8 7.4 fusion.5
  441.3 8.5 %fusion.6 = f32[1088,3264]{1,0:T(8,128)} fusion(f32[1088,3264]{1,0:T(8,128)S(1)} %fusion.5, pred[]{:T(512)S(6)} %lt.170, bf16[64,1088]{0,1:T(8,128)(2,1)S(1)} %bitcast.562, bf16[64,1088]{0,1:T(8,128)(2,1)S(1)} %bitcast.600, bf16[64,1088]{0,1:T(8,128)(2,1)S(1)} %bitcast.560, bf16[3,64,1088]{1,2,0:T(8,128)(2,1)} %constant_dynamic-update-slice_fusion.6, ...), kind=kOutput, calls=%fused_computation.7 | convolution fusion | flops 462913536 | bytes 29106180 | tf_op jit(solution)/shard_map/dot_general | solution.py:55
  449.7 5.8 fusion.12
  455.6 234.1 %fusion.348 = (f32[72,3264]{1,0:T(8,128)S(1)}, f32[80,1088]{1,0:T(8,128)S(1)}) fusion(f32[1088,3264]{1,0:T(8,128)} %fusion.6, f32[1088,1088]{1,0:T(8,128)} %fusion.12), kind=kCustom, calls=%all-reduce-scatter.2 | all-reduce-scatter fusion | flops 5152770 | bytes 20228608
  690.5 21.4 %collective-permute-start.6 = (f32[80,1088]{1,0:T(8,128)S(1)}, f32[80,1088]{1,0:T(8,128)S(1)}, u32[]{:S(2)}, u32[]{:S(2)}) collective-permute-start(f32[80,1088]{1,0:T(8,128)S(1)} %get-tuple-element.84), channel_id=1, source_target_pairs={{0,2},{1,3},{2,4},{3,5},{4,6},{5,7},{6,8},{7,9},{8,10},{9,11},{10,... | collective-permute-start | bytes 1044488
  719.2 61.1 %all-reduce.8 = (f32[2,1088]{1,0:T(2,128)S(1)}, f32[6,1088]{1,0:T(8,128)S(1)}) all-reduce(f32[2,1088]{1,0:T(2,128)S(1)} %fusion.307, f32[6,1088]{1,0:T(8,128)S(1)} %select_add_fusion), channel_id=11, replica_groups=mesh['section'=2,'dp'=4,'tensor'=4] {'dp','tensor'}, use_global_device_ids=true, to_apply=%region_59.60.clone | all-reduce | flops 8704 | bytes 69632
  790.3 7.1 concatenate.27
  (628 shorter events, 327.6 us)
Async XLA Ops:
  7.2 31.3 %copy-start = (bf16[1,1088,1088]{2,1,0:T(8,128)(2,1)S(1)}, bf16[1,1088,1088]{2,1,0:T(8,128)(2,1)}, u32[]{:S(2)}) copy-start(bf16[1,1088,1088]{2,1,0:T(8,128)(2,1)} %param.14) | copy-start | bytes 7102468
  7.2 84.4 %reduce-scatter.13.cloned.1.call-start = ((), (), s32[]{:S(2)}) async-start(), calls=%async_computation.6 | async-start | bytes 737280 | tf_op jit(solution)/shard_map/reduce_scatter | solution.py:112
  44.9 113.8 %reduce-scatter.15.cloned.1.call-start = ((), (), s32[]{:S(2)}) async-start(), calls=%async_computation.7 | async-start | bytes 737280 | tf_op jit(solution)/shard_map/reduce_scatter | solution.py:112
  92.5 7.1 collective-permute-start
  134.7 108.0 %reduce-scatter.19.cloned.1.call-start = ((), (), s32[]{:S(2)}) async-start(), calls=%async_computation.9 | async-start | bytes 737280 | tf_op jit(solution)/shard_map/reduce_scatter | solution.py:164
  159.6 6.3 collective-permute-start.1
  217.7 55.4 %reduce-scatter.17.cloned.1.call-start = ((), (), s32[]{:S(2)}) async-start(), calls=%async_computation.8 | async-start | bytes 737280 | tf_op jit(solution)/shard_map/reduce_scatter | solution.py:112
  224.7 95.3 %reduce-scatter.21.cloned.1.call-start = ((), (), s32[]{:S(2)}) async-start(), calls=%async_computation.10 | async-start | bytes 737280 | tf_op jit(solution)/shard_map/reduce_scatter | solution.py:164
  271.8 8.1 collective-permute-start.2
  295.5 107.0 %reduce-scatter.23.cloned.1.call-start = ((), (), s32[]{:S(2)}) async-start(), calls=%async_computation.11 | async-start | bytes 737280 | tf_op jit(solution)/shard_map/reduce_scatter | solution.py:164
  351.3 8.1 collective-permute-start.3
  374.8 425.9 %all-reduce.13.cloned.1.call-start = ((), (), s32[]{:S(2)}) async-start(), calls=%async_computation.12 | async-start | bytes 10027008 | tf_op jit(solution)/shard_map/psum | solution.py:293
  455.6 258.3 %copy-start.93 = (f32[1088]{0:T(1024)S(1)}, f32[1088]{0:T(1024)}, u32[]{:S(2)}) copy-start(f32[1088]{0:T(1024)} %get-tuple-element.51) | copy-start | bytes 13060
  455.6 258.3 %copy-start.94 = (f32[1088]{0:T(1024)S(1)}, f32[1088]{0:T(1024)}, u32[]{:S(2)}) copy-start(f32[1088]{0:T(1024)} %get-tuple-element.95) | copy-start | bytes 13060
  455.6 258.3 %copy-start.92 = (f32[1088]{0:T(1024)S(1)}, f32[1088]{0:T(1024)}, u32[]{:S(2)}) copy-start(f32[1088]{0:T(1024)} %get-tuple-element.68) | copy-start | bytes 13060
  455.6 258.4 %copy-start.110 = (f32[17,64]{1,0:T(8,128)S(1)}, f32[17,64]{1,0:T(8,128)}, u32[]{:S(2)}) copy-start(f32[17,64]{1,0:T(8,128)} %get-tuple-element.132) | copy-start | bytes 13060
  455.6 258.5 %copy-start.95 = (f32[1088]{0:T(1024)S(1)}, f32[1088]{0:T(1024)}, u32[]{:S(2)}) copy-start(f32[1088]{0:T(1024)} %get-tuple-element.141) | copy-start | bytes 13060
  689.8 29.4 %copy-start.100 = (f32[1,1088]{1,0:T(1,128)S(1)}, f32[1,1088]{1,0:T(1,128)}, u32[]{:S(2)}) copy-start(f32[1,1088]{1,0:T(1,128)} %stack.91) | copy-start | bytes 13060
  689.8 29.4 %copy-start.101 = (f32[1,1088]{1,0:T(1,128)S(1)}, f32[1,1088]{1,0:T(1,128)}, u32[]{:S(2)}) copy-start(f32[1,1088]{1,0:T(1,128)} %stack.90) | copy-start | bytes 13060
  690.5 95.5 %collective-permute-start.6 = (f32[80,1088]{1,0:T(8,128)S(1)}, f32[80,1088]{1,0:T(8,128)S(1)}, u32[]{:S(2)}, u32[]{:S(2)}) collective-permute-start(f32[80,1088]{1,0:T(8,128)S(1)} %get-tuple-element.84), channel_id=1, source_target_pairs={{0,2},{1,3},{2,4},{3,5},{4,6},{5,7},{6,8},{7,9},{8,10},{9,11},{10,... | collective-permute-start | bytes 1044488
  711.8 74.9 %collective-permute-start.5 = (f32[80,1088]{1,0:T(8,128)S(1)}, f32[80,1088]{1,0:T(8,128)}, u32[]{:S(2)}, u32[]{:S(2)}) collective-permute-start(f32[80,1088]{1,0:T(8,128)S(1)} %get-tuple-element.84), channel_id=1, source_target_pairs={{0,1},{1,2},{2,3},{3,4},{4,5},{5,6},{6,7},{7,8},{8,9},{9,10},{10,1... | collective-permute-start | bytes 1044488
  714.1 67.0 %copy-start.33 = (bf16[3,64,1088]{1,2,0:T(8,128)(2,1)S(1)}, bf16[3,64,1088]{1,2,0:T(8,128)(2,1)}, u32[]{:S(2)}) copy-start(bf16[3,64,1088]{1,2,0:T(8,128)(2,1)} %constant_dynamic-update-slice_fusion.10) | copy-start | bytes 1253380
  715.1 75.3 %collective-permute-start.4 = (f32[60,3264]{1,0:T(8,128)}, f32[60,3264]{1,0:T(8,128)}, u32[]{:S(2)}, u32[]{:S(2)}) collective-permute-start(f32[60,3264]{1,0:T(8,128)} %slice.128), channel_id=1, source_target_pairs={{0,1},{1,2},{2,3},{3,4},{4,5},{5,6},{6,7},{7,8},{8,9},{9,10},{10,1... | collective-permute-start | bytes 2350088
  782.4 3.6 collective-permute-start.7
  (143 other events, 956.2 us)
Sparse Core Ops, SparseCore 0:
  45.0 22.9 reduce-scatter.12
  134.9 23.7 reduce-scatter.14
  217.9 24.8 reduce-scatter.18
  245.1 22.0 reduce-scatter.16
  295.7 23.5 reduce-scatter.20
  374.9 21.4 reduce-scatter.22
  402.7 229.2 all-reduce.12
where the time goes:
time: 826 us; the launch traced here: 815 us
  blocking collectives  353 us (43%)
  matrix products  166 us (20%)
  local copies, waits for them, and re-layouts  152 us (18%)
  other arithmetic  56.6 us (7%)
  starting transfers between devices  38.6 us (5%)
  waiting for transfers between devices  29.5 us (4%)
  between operations  18.2 us (2%)
    unnamed x2, blocking collectives  295 us
    dot_general x12, matrix products, contract_rows(): lax.dot_general(left, right, (((0,), (0,)), ((), ())), preferred_element_...  63.9 us
    dot_general x12, matrix products, contract_cols(): lax.dot_general(left, right, (((1,), (1,)), ((), ())), preferred_element_...  41 us
    unnamed x316, local copies, waits for them, and re-layouts  30.9 us
    unnamed x4, starting transfers between devices  27.5 us
    broadcast_in_dim x17, local copies, waits for them, and re-layouts, per_device(): lax.dynamic_update_index_in_dim(whole_buf, new_part, slot_index, 0)  25.2 us
    dynamic_update_slice x21, local copies, waits for them, and re-layouts, per_device(): lax.dynamic_update_index_in_dim(whole_buf, new_part, slot_index, 0)  24.6 us
    all_gather x3, blocking collectives, layer_forward(): gathered = lax.all_gather(normal_two, 'tensor', axis=0, tiled=True)  23.8 us
  transfers between devices with their start and end apart: 15, of which 6 were waited for; matrix products, arithmetic and copies ran while one was open for 55% of the time, Pallas kernels for 0%

commit v1 on v0

v1 whole, which is shorter than its diff:
```python
import math

import jax
import jax.numpy as jnp
from jax import lax
from jax.sharding import PartitionSpec as P

HEADS = 17


EPSILON = 1e-05
GELU_SCALE = math.sqrt(2.0 / math.pi)
GELU_CUBIC = 0.044715


def shifted(block, axis, distance):
    devices = range(lax.axis_size(axis))
    route = [(i - distance, i) for i in devices if i - distance in devices]
    return lax.ppermute(block, axis, route)


def norm_rows(values):
    centre = values - jnp.mean(values, axis=-1, keepdims=True)
    inverse = lax.rsqrt(jnp.mean(centre * centre, axis=-1, keepdims=True) + EPSILON)
    return (centre * inverse, inverse)


def norm_back(grad_normed, normed, inverse, gain):
    scaled = grad_normed * gain
    return (
        scaled
        - jnp.mean(scaled, axis=-1, keepdims=True)
        - normed * jnp.mean(scaled * normed, axis=-1, keepdims=True)
    ) * inverse


def gelu_tanh(values):
    return (
        0.5
        * values
        * (1.0 + jnp.tanh(GELU_SCALE * (values + GELU_CUBIC * values * values * values)))
    )


def gelu_slope(values):
    tangent = jnp.tanh(GELU_SCALE * (values + GELU_CUBIC * values * values * values))
    return 0.5 * (1.0 + tangent) + 0.5 * values * (1.0 - tangent * tangent) * GELU_SCALE * (
        1.0 + 3.0 * GELU_CUBIC * values * values
    )


def contract_rows(left, right):
    return lax.dot_general(
        left, right, (((0,), (0,)), ((), ())), preferred_element_type=jnp.float32
    )


def contract_cols(left, right):
    return lax.dot_general(
        left, right, (((1,), (1,)), ((), ())), preferred_element_type=jnp.float32
    )


def make_segments(seq_lengths, row_count):
    block_count = seq_lengths.shape[0]
    block_rows = row_count // block_count
    ends = jnp.cumsum(seq_lengths.astype(jnp.int32), axis=1)
    starts = jnp.arange(block_count, dtype=jnp.int32)[:, None] * block_rows
    ends = (ends + starts).reshape(-1)
    places = jnp.arange(row_count, dtype=jnp.int32)
    segment = jnp.sum((places[:, None] >= ends[None, :]).astype(jnp.int32), axis=1)
    return (segment[:, None] == segment[None, :]) & (places[None, :] <= places[:, None])


def head_split(values):
    return values.reshape(values.shape[0], HEADS, values.shape[1] // HEADS).transpose(1, 0, 2)


def head_join(values):
    return values.transpose(1, 0, 2).reshape(values.shape[1], -1)


def batched(left, right, left_dim, right_dim):
    return lax.dot_general(
        left,
        right,
        (((left_dim,), (right_dim,)), ((0,), (0,))),
        preferred_element_type=jnp.float32,
    )


def gather_all(rows):
    over_dp = lax.all_gather(rows, "dp", axis=0, tiled=True)
    return lax.all_gather(over_dp, "tensor", axis=0, tiled=True)


def layer_forward(layer_in, allowed, params):
    w_qkv, w_out, w_up, up_bias, w_down, gains, biases = params
    row_count, model_width = layer_in.shape
    head_width = model_width // HEADS
    inflow = layer_in.astype(jnp.float32)
    normed_one, inverse_one = norm_rows(inflow)
    normal_one = (normed_one * gains[0] + biases[0]).astype(jnp.bfloat16)
    projected = jnp.dot(normal_one, w_qkv, preferred_element_type=jnp.float32)
    queries = head_split((projected[:, :model_width] + biases[1]).astype(jnp.bfloat16))
    keys_all = head_split(projected[:, model_width : 2 * model_width].astype(jnp.bfloat16))
    values_all = head_split((projected[:, 2 * model_width :] + biases[2]).astype(jnp.bfloat16))
    scores = batched(queries, keys_all, 2, 2) * head_width ** (-0.5)
    masked = jnp.where(allowed[None], scores, -jnp.inf)
    peak = jnp.max(masked, axis=-1, keepdims=True)
    raised = jnp.exp(masked - peak)
    probs_f = raised / jnp.sum(raised, axis=-1, keepdims=True)
    probs = probs_f.astype(jnp.bfloat16)
    mixed = head_join(batched(probs, values_all, 2, 1)).astype(jnp.bfloat16)
    residual = inflow + jnp.dot(mixed, w_out, preferred_element_type=jnp.float32) + biases[3]
    normed_two, inverse_two = norm_rows(residual)
    normal_two = (normed_two * gains[1] + biases[4]).astype(jnp.bfloat16)
    gathered = lax.all_gather(normal_two, "tensor", axis=0, tiled=True)
    hidden_pre = jnp.dot(gathered, w_up, preferred_element_type=jnp.float32) + up_bias
    hidden = gelu_tanh(hidden_pre).astype(jnp.bfloat16)
    branch = lax.psum_scatter(
        jnp.dot(hidden, w_down, preferred_element_type=jnp.float32).astype(jnp.bfloat16),
        "tensor",
        scatter_dimension=0,
        tiled=True,
    ).astype(jnp.float32)
    result = (residual + branch + biases[5]).astype(jnp.bfloat16)
    kept = (
        normal_one,
        normed_one,
        inverse_one,
        queries,
        keys_all,
        values_all,
        mixed,
        probs_f,
        normed_two,
        inverse_two,
        normal_two,
        hidden_pre,
    )
    return (result, kept)


def layer_backward(grad_out, kept, params):
    w_qkv, w_out, w_up, up_bias, w_down, gains, biases = params
    (
        normal_one,
        normed_one,
        inverse_one,
        queries,
        keys_all,
        values_all,
        mixed,
        probs_f,
        normed_two,
        inverse_two,
        normal_two,
        hidden_pre,
    ) = kept
    row_count, model_width = grad_out.shape
    head_width = model_width // HEADS
    grad_flow = grad_out.astype(jnp.float32)
    grad_rows = lax.all_gather(grad_out, "tensor", axis=0, tiled=True)
    grad_hidden = contract_cols(grad_rows, w_down)
    grad_pre = grad_hidden * gelu_slope(hidden_pre)
    grad_pre_b = grad_pre.astype(jnp.bfloat16)
    grad_two = lax.psum_scatter(
        contract_cols(grad_pre_b, w_up).astype(jnp.bfloat16),
        "tensor",
        scatter_dimension=0,
        tiled=True,
    ).astype(jnp.float32)
    grad_resid = grad_flow + norm_back(grad_two, normed_two, inverse_two, gains[1])
    grad_resid_b = grad_resid.astype(jnp.bfloat16)
    grad_mixed = head_split(contract_cols(grad_resid_b, w_out).astype(jnp.bfloat16))
    probs_b = probs_f.astype(jnp.bfloat16)
    grad_probs = batched(grad_mixed, values_all, 2, 2)
    grad_values = head_join(batched(probs_b, grad_mixed, 1, 1))
    centre = jnp.sum(probs_f * grad_probs, axis=-1, keepdims=True)
    grad_scores = (probs_f * (grad_probs - centre) * head_width ** (-0.5)).astype(jnp.bfloat16)
    grad_queries = head_join(batched(grad_scores, keys_all, 2, 1))
    grad_keys = head_join(batched(grad_scores, queries, 1, 1))
    grad_proj = jnp.concatenate([grad_queries, grad_keys, grad_values], axis=1).astype(jnp.bfloat16)
    grad_one = contract_cols(grad_proj, w_qkv)
    grad_in = (grad_resid + norm_back(grad_one, normed_one, inverse_one, gains[0])).astype(
        jnp.bfloat16
    )

    def feed_grads():
        inputs_all = gather_all(normal_two)
        grads_all = gather_all(grad_out)
        pre_all = jnp.dot(inputs_all, w_up, preferred_element_type=jnp.float32) + up_bias
        hidden_all = gelu_tanh(pre_all).astype(jnp.bfloat16)
        grad_all = contract_cols(grads_all, w_down) * gelu_slope(pre_all)
        return (
            contract_rows(inputs_all, grad_all.astype(jnp.bfloat16)),
            contract_rows(hidden_all, grads_all),
            jnp.sum(grad_all, axis=0),
        )

    def token_grads():
        small = jnp.stack(
            [
                jnp.sum(normed_one * grad_one, axis=0),
                jnp.sum(normed_two * grad_two, axis=0),
                jnp.sum(grad_one, axis=0),
                jnp.sum(grad_queries, axis=0),
                jnp.sum(grad_values, axis=0),
                jnp.sum(grad_resid, axis=0),
                jnp.sum(grad_two, axis=0),
                jnp.sum(grad_flow, axis=0),
            ]
        )
        return (
            contract_rows(normal_one, grad_proj),
            contract_rows(mixed, grad_resid_b),
            small,
        )

    return (grad_in, feed_grads, token_grads)


def per_device(tokens, lengths, w_qkv, w_out, w_up, up_bias, w_down, gains, biases, cotangent):
    section_index = lax.axis_index("section")
    row_count, model_width = tokens.shape
    params = (w_qkv[0], w_out[0], w_up[0], up_bias[0], w_down[0], gains[0], biases[0])
    allowed = make_segments(lengths[0], row_count)
    first_result, _ = layer_forward(tokens, allowed, params)
    arrived = shifted(first_result, "section", 1)
    layer_in = jnp.where(section_index == 0, tokens, arrived)
    result, kept = layer_forward(layer_in, allowed, params)
    first_grad, _, _ = layer_backward(cotangent, kept, params)
    grad_arrived = shifted(first_grad, "section", -1)
    grad_out = jnp.where(section_index == 1, cotangent, grad_arrived)
    grad_in, feed_grads, token_grads = layer_backward(grad_out, kept, params)

    grad_up, grad_down, grad_up_bias = feed_grads()
    grad_wqkv, grad_wout, small = token_grads()
    owners = lax.axis_size(("dp", "tensor"))
    piece = model_width // owners
    joined = jnp.concatenate([grad_wqkv, grad_wout, small.T], axis=1).astype(jnp.bfloat16)
    joined = lax.psum_scatter(
        joined.reshape(owners, piece, -1), ("dp", "tensor"), scatter_dimension=0
    ).astype(jnp.float32)
    qkv_width = grad_wqkv.shape[1]
    small = joined[:, qkv_width + model_width :].T
    return (
        result[None],
        grad_in[None],
        joined[None, :, :qkv_width],
        joined[None, :, qkv_width : qkv_width + model_width],
        small[None, :2],
        small[None, 2:],
        grad_up[None],
        grad_up_bias[None],
        grad_down[None],
    )


def solution(mesh):
    in_specs = (
        P(("dp", "tensor"), None),
        P(("dp", "tensor"), None, None),
        P("section", None, None),
        P("section", None, None),
        P("section", None, "tensor"),
        P("section", "tensor"),
        P("section", "tensor", None),
        P("section", None, None),
        P("section", None, None),
        P(("dp", "tensor"), None),
    )
    out_specs = (
        P("section", ("dp", "tensor"), None),
        P("section", ("dp", "tensor"), None),
        P("section", ("dp", "tensor"), None),
        P("section", ("dp", "tensor"), None),
        P("section", None, ("dp", "tensor")),
        P("section", None, ("dp", "tensor")),
        P("section", None, "tensor"),
        P("section", "tensor"),
        P("section", "tensor", None),
    )
    return jax.shard_map(
        per_device, mesh=mesh, in_specs=in_specs, out_specs=out_specs, check_vma=False
    )
```

time: 826 us -> 579 us (0.70)
  blocking collectives: 353 us -> 0 us
  waiting for transfers between devices: 29.5 us -> 313 us
  local copies, waits for them, and re-layouts: 152 us -> 53.7 us
  other arithmetic: 56.6 us -> 22.1 us
  starting transfers between devices: 38.6 us -> 17 us
  matrix products: 166 us -> 148 us
    unnamed x2 -> x0, blocking collectives: 295 us -> none
    unnamed x11 -> x18, waiting for transfers between devices: 1.79 us -> 185 us
    all_gather x0 -> x8, waiting for transfers between devices: none -> 114 us  [the longest x2 54.6 us: gather_all(): over_dp = lax.all_gather(rows, 'dp', axis=0, tiled=True)]
    all_gather x6 -> x0, blocking collectives: 46 us -> none  [the longest x3 23.8 us: layer_forward(): gathered = lax.all_gather(normal_two, 'tensor', axis=0, tiled=True)]
    dot_general x12 -> x4, matrix products: 63.9 us -> 26.9 us  [contract_rows(): lax.dot_general(left, right, (((0,), (0,)), ((), ())), preferred_element_...]
    another operation x47 -> x9, local copies, waits for them, and re-layouts: 36.5 us -> 0.28 us  [token_grads(): jnp.stack([jnp.sum(normed_one * grad_one, axis=0), jnp.sum(normed_two * g...]
    broadcast_in_dim x30 -> x5, local copies, waits for them, and re-layouts: 31.2 us -> 0.88 us  [the longest x1 0.6 us: per_device(): grad_up_bias[None]]
    dynamic_update_slice x27 -> x0, local copies, waits for them, and re-layouts: 27.9 us -> none  [the longest x21 24.6 us: per_device(): lax.dynamic_update_index_in_dim(whole_buf, new_part, slot_index, 0)]
  transfers between devices with their start and end apart: 15 -> 15, of which waited for: 6 -> 14; matrix products, arithmetic and copies ran while one was open for 55% -> 23% of each run, Pallas kernels for 0% -> 0%
where the time goes in v1:
time: 579 us; the launch traced here: 569 us
  waiting for transfers between devices  313 us (54%)
  matrix products  148 us (26%)
  local copies, waits for them, and re-layouts  53.7 us (9%)
  other arithmetic  22.1 us (4%)
  starting transfers between devices  17 us (3%)
  between operations  14.7 us (3%)
    unnamed x18, waiting for transfers between devices  185 us
    all_gather x2, waiting for transfers between devices, gather_all(): over_dp = lax.all_gather(rows, 'dp', axis=0, tiled=True)  54.6 us
    dot_general x7, matrix products, contract_cols(): lax.dot_general(left, right, (((1,), (1,)), ((), ())), preferred_element_...  42.4 us
    all_gather x2, waiting for transfers between devices, layer_forward(): gathered = lax.all_gather(normal_two, 'tensor', axis=0, tiled=True)  36.7 us
    dot_general x11, matrix products, batched(): lax.dot_general(left, right, (((left_dim,), (right_dim,)), ((0,), (0,))),...  29.8 us
    dot_general x4, matrix products, contract_rows(): lax.dot_general(left, right, (((0,), (0,)), ((), ())), preferred_element_...  26.9 us
    concatenate x4, local copies, waits for them, and re-layouts, per_device(): jnp.concatenate([grad_wqkv, grad_wout, small.T], axis=1)  26.2 us
    unnamed x50, local copies, waits for them, and re-layouts  21.8 us
  transfers between devices with their start and end apart: 15, of which 14 were waited for; matrix products, arithmetic and copies ran while one was open for 23% of the time, Pallas kernels for 0%

profile of v1, /device:TPU:0, one launch (start us, length us, event | category | flops | bytes accessed | tf_op | source)
XLA Modules:
  0.0 568.5 jit_solution(4439945965232558597)
XLA Ops:
  11.3 6.5 %fusion.15 = f32[128,3264]{0,1:T(8,128)S(1)} fusion(bf16[1,1088,3264]{2,1,0:T(8,128)(2,1)} %param.12, bf16[128,1088]{0,1:T(8,128)(2,1)} %param.10, f32[1088]{0:T(1024)S(1)} %get-tuple-element.51, f32[1088]{0:T(1024)S(1)} %get-tuple-element.54, f32[128]{0:T(128)S(1)} %add_rsqrt_fusion.3, f32[128]{0:T(128)S(1)} %broadcast_multiply_fusion.11), kind=kOutput, calls=%fused_computation.23 | convolution fusion | flops 909950976 | bytes 9061888 | tf_op jit(solution)/shard_map/dot_general | solution.py:104
  30.9 20.0 %all-gather.9.cloned.1.call-done = bf16[512,1088]{0,1:T(8,128)(2,1)} async-done(((bf16[128,1088]{0,1:T(8,128)(2,1)}), bf16[512,1088]{0,1:T(8,128)(2,1)}) %all-gather.9.cloned.1.call-update) | async-done | bytes 1114128 | tf_op jit(solution)/shard_map/all_gather | solution.py:118
  50.9 6.5 %convolution_convert_fusion.5 = bf16[512,1088]{0,1:T(8,128)(2,1)} fusion(bf16[1,1088,1088]{2,1,0:T(8,128)(2,1)S(1)} %copy-done, bf16[512,1088]{0,1:T(8,128)(2,1)} %all-gather.9.cloned.1.call-done, bf16[1,1088,1088]{2,1,0:T(8,128)(2,1)} %param.14, f32[1088]{0:T(1024)S(1)} %reduce.11), kind=kOutput, calls=%fused_computation.43 | convolution fusion | flops 2430435328 | bytes 6967552 | tf_op jit(solution)/shard_map/dot_general | solution.py:122
  59.9 25.7 %reduce-scatter.16.cloned.1.call-done = bf16[128,1088]{1,0:T(8,128)(2,1)} async-done(((bf16[512,1088]{1,0:T(8,128)(2,1)}), bf16[128,1088]{1,0:T(8,128)(2,1)}) %reduce-scatter.16.cloned.1.call-update) | async-done | bytes 278544
  98.4 6.4 %fusion.13 = f32[128,3264]{0,1:T(8,128)S(1)} fusion(bf16[1,1088,3264]{2,1,0:T(8,128)(2,1)} %param.12, bf16[128,1088]{0,1:T(8,128)(2,1)S(1)} %get-tuple-element.60, f32[128]{0:T(128)S(1)} %add_rsqrt_fusion.1, f32[128]{0:T(128)S(1)} %broadcast_multiply_fusion.9, f32[1088]{0:T(1024)S(1)} %get-tuple-element.51, f32[1088]{0:T(1024)S(1)} %get-tuple-element.54), kind=kOutput, calls=%fused_computation.21 | convolution fusion | flops 909950976 | bytes 9061888 | tf_op jit(solution)/shard_map/dot_general | solution.py:104
  115.7 16.7 %all-gather.11.cloned.1.call-done = bf16[512,1088]{0,1:T(8,128)(2,1)} async-done(((bf16[128,1088]{0,1:T(8,128)(2,1)}), bf16[512,1088]{0,1:T(8,128)(2,1)}) %all-gather.11.cloned.1.call-update) | async-done | bytes 1114128 | tf_op jit(solution)/shard_map/all_gather | solution.py:118
  137.5 13.6 %all-gather.13.cloned.1.call-done = bf16[512,1088]{0,1:T(8,128)(2,1)} async-done(((bf16[128,1088]{0,1:T(8,128)(2,1)}), bf16[512,1088]{0,1:T(8,128)(2,1)}) %all-gather.13.cloned.1.call-update) | async-done | bytes 1114128 | tf_op jit(solution)/shard_map/all_gather | solution.py:164
  151.0 7.3 %convolution_convert_fusion.3 = bf16[512,1088]{0,1:T(8,128)(2,1)} fusion(bf16[1,1088,1088]{2,1,0:T(8,128)(2,1)} %param.14, bf16[512,1088]{0,1:T(8,128)(2,1)} %all-gather.13.cloned.1.call-done, bf16[1,1088,1088]{2,1,0:T(8,128)(2,1)S(1)} %copy-done, f32[512,1088]{0,1:T(8,128)} %convolution_add_fusion.1), kind=kOutput, calls=%fused_computation.41 | convolution fusion | flops 2435448832 | bytes 9191424 | tf_op jit(solution)/shard_map/dot_general | solution.py:59
  160.7 11.6 %all-gather.15.cloned.1.call-start = ((), (), s32[]{:S(2)}) async-start(), calls=%async_computation.8 | async-start | bytes 1392640 | tf_op jit(solution)/shard_map/all_gather | solution.py:164
  172.3 14.2 %reduce-scatter.20.cloned.1.call-done = bf16[128,1088]{1,0:T(8,128)(2,1)} async-done(((bf16[512,1088]{1,0:T(8,128)(2,1)}), bf16[128,1088]{1,0:T(8,128)(2,1)}) %reduce-scatter.20.cloned.1.call-update) | async-done | bytes 278544
  212.7 9.2 %collective-permute-done.1 = bf16[128,1088]{0,1:T(8,128)(2,1)} collective-permute-done((bf16[128,1088]{0,1:T(8,128)(2,1)}, bf16[128,1088]{0,1:T(8,128)(2,1)}, u32[]{:S(2)}, u32[]{:S(2)}) %collective-permute-start.1) | collective-permute-done | bytes 278560 | tf_op jit(solution)/shard_map/ppermute | solution.py:19
  232.1 8.0 %all-gather.15.cloned.1.call-done = bf16[512,1088]{0,1:T(8,128)(2,1)} async-done(((bf16[128,1088]{0,1:T(8,128)(2,1)}), bf16[512,1088]{0,1:T(8,128)(2,1)}) %all-gather.15.cloned.1.call-update) | async-done | bytes 1114128 | tf_op jit(solution)/shard_map/all_gather | solution.py:164
  240.1 7.3 %convolution_convert_fusion.2 = bf16[512,1088]{0,1:T(8,128)(2,1)} fusion(bf16[1,1088,1088]{2,1,0:T(8,128)(2,1)} %param.14, bf16[512,1088]{0,1:T(8,128)(2,1)} %all-gather.15.cloned.1.call-done, bf16[1,1088,1088]{2,1,0:T(8,128)(2,1)S(1)} %copy-done, f32[512,1088]{0,1:T(8,128)} %convolution_add_fusion.1), kind=kOutput, calls=%fused_computation.40 | convolution fusion | flops 2435448832 | bytes 9191424 | tf_op jit(solution)/shard_map/dot_general | solution.py:59
  249.9 23.3 %all-gather.17.cloned.1.call-done = bf16[512,1088]{0,1:T(8,128)(2,1)} async-done(((bf16[128,1088]{0,1:T(8,128)(2,1)}), bf16[512,1088]{0,1:T(8,128)(2,1)}) %all-gather.17.cloned.1.call-update) | async-done | bytes 1114128 | tf_op jit(solution)/shard_map/all_gather | solution.py:93
  273.2 31.3 %all-gather.21.cloned.1.call-done = bf16[512,1088]{0,1:T(8,128)(2,1)} async-done(((bf16[128,1088]{0,1:T(8,128)(2,1)}), bf16[512,1088]{0,1:T(8,128)(2,1)}) %all-gather.21.cloned.1.call-update) | async-done | bytes 1114128 | tf_op jit(solution)/shard_map/all_gather | solution.py:93
  306.3 25.3 %reduce-scatter.18.cloned.1.call-done = bf16[128,1088]{1,0:T(8,128)(2,1)} async-done(((bf16[512,1088]{1,0:T(8,128)(2,1)}), bf16[128,1088]{1,0:T(8,128)(2,1)}) %reduce-scatter.18.cloned.1.call-update) | async-done | bytes 278544
  333.4 26.8 %reduce-scatter.22.cloned.1.call-done = bf16[128,1088]{1,0:T(8,128)(2,1)} async-done(((bf16[512,1088]{1,0:T(8,128)(2,1)}), bf16[128,1088]{1,0:T(8,128)(2,1)}) %reduce-scatter.22.cloned.1.call-update) | async-done | bytes 278544
  384.5 9.1 %concatenate.19 = bf16[16,68,3264]{2,1,0:T(8,128)(2,1)} reshape(bf16[1088,3264]{1,0:T(8,128)(2,1)} %convolution_convert_fusion) | data formatting | bytes 14204928 | tf_op jit(solution)/shard_map/concatenate | solution.py:242
  405.6 16.1 %concatenate.21 = bf16[16,68,4360]{2,1,0:T(8,128)(2,1)} concatenate(bf16[16,68,3264]{2,1,0:T(8,128)(2,1)} %concatenate.19, bf16[16,68,1088]{2,1,0:T(8,128)(2,1)} %convolution_convert_fusion.1, bf16[16,68,8]{2,1,0:T(8,128)(2,1)} %copy.63), dimensions={2} | concatenate | bytes 18974720 | tf_op jit(solution)/shard_map/concatenate | solution.py:242
  423.7 10.6 %convolution_add_fusion = f32[2048,1088]{0,1:T(8,128)} fusion(bf16[2048,1088]{0,1:T(8,128)(2,1)} %all-gather.19.cloned.1.call-done, f32[1088]{0:T(1024)S(1)} %reduce.11, bf16[1,1088,1088]{2,1,0:T(8,128)(2,1)} %param.14), kind=kOutput, calls=%fused_computation.8 | convolution fusion | flops 4850843648 | bytes 15741184 | tf_op jit(solution)/shard_map/dot_general | solution.py:193
  435.2 12.0 %fusion.207 = (f32[1088]{0:T(1024)S(1)}, bf16[2048,1088]{0,1:T(8,128)(2,1)S(1)}) fusion(f32[2048,1088]{0,1:T(8,128)} %convolution_add_fusion, bf16[2048,1088]{0,1:T(8,128)(2,1)} %all-gather.23.cloned.1.call-done, bf16[1,1088,1088]{2,1,0:T(8,128)(2,1)S(1)} %copy-done), kind=kOutput, calls=%fused_computation.275 | convolution fusion | flops 4893178880 | bytes 20197632 | tf_op jit(solution)/shard_map/dot_general | solution.py:59
  447.8 7.9 %convolution_bitcast_fusion.1 = f32[1,1088,1088]{2,1,0:T(8,128)} fusion(bf16[2048,1088]{0,1:T(8,128)(2,1)S(1)} %copy-done.14, bf16[2048,1088]{0,1:T(8,128)(2,1)S(1)} %get-tuple-element.81), kind=kOutput, calls=%fused_computation.16 | convolution fusion | flops 4848615424 | bytes 13647872 | tf_op jit(solution)/shard_map/dot_general | solution.py:53
  455.8 9.3 %convolution_bitcast_fusion = f32[1,1088,1088]{2,1,0:T(8,128)} fusion(bf16[2048,1088]{0,1:T(8,128)(2,1)S(1)} %copy-done.15, f32[2048,1088]{0,1:T(8,128)S(1)} %bitcast.223), kind=kOutput, calls=%fused_computation.15 | convolution fusion | flops 4868669440 | bytes 18104320 | tf_op jit(solution)/shard_map/dot_general | solution.py:53
  465.1 90.8 %reduce-scatter.24.cloned.1.call-done = bf16[1,68,4360]{2,1,0:T(8,128)(2,1)} async-done(((bf16[16,68,4360]{2,1,0:T(8,128)(2,1)}), bf16[1,68,4360]{2,1,0:T(8,128)(2,1)}) %reduce-scatter.24.cloned.1.call-update) | async-done | bytes 592976
  (167 shorter events, 138.4 us)
Async XLA Ops:
  7.2 43.7 %copy-start = (bf16[1,1088,1088]{2,1,0:T(8,128)(2,1)S(1)}, bf16[1,1088,1088]{2,1,0:T(8,128)(2,1)}, u32[]{:S(2)}) copy-start(bf16[1,1088,1088]{2,1,0:T(8,128)(2,1)} %param.16) | copy-start | bytes 7102468
  7.2 43.7 %all-gather.9.cloned.1.call-start = ((), (), s32[]{:S(2)}) async-start(), calls=%async_computation.5 | async-start | bytes 1392640 | tf_op jit(solution)/shard_map/all_gather | solution.py:118
  11.3 7.7 %copy-start.13 = (s32[1,2,4]{2,1,0:T(2,128)S(1)}, s32[1,2,4]{2,1,0:T(2,128)}, u32[]{:S(2)}) copy-start(s32[1,2,4]{2,1,0:T(2,128)} %param.11) | copy-start | bytes 100
  30.8 54.8 %reduce-scatter.16.cloned.1.call-start = ((), (), s32[]{:S(2)}) async-start(), calls=%async_computation.13 | async-start | bytes 1474560
  59.8 72.5 %all-gather.11.cloned.1.call-start = ((), (), s32[]{:S(2)}) async-start(), calls=%async_computation.6 | async-start | bytes 1392640 | tf_op jit(solution)/shard_map/all_gather | solution.py:118
  87.7 9.4 %collective-permute-start = (bf16[128,1088]{0,1:T(8,128)(2,1)}, bf16[128,1088]{0,1:T(8,128)(2,1)S(1)}, u32[]{:S(2)}, u32[]{:S(2)}) collective-permute-start(bf16[128,1088]{0,1:T(8,128)(2,1)} %add_convert_fusion.2), channel_id=1, source_target_pairs={{0,16},{1,17},{2,18},{3,19},{4,20},{5,21},{6,22},{7,23},{8,24},{9,... | collective-permute-start | bytes 835592 | tf_op jit(solution)/shard_map/ppermute | solution.py:19
  105.2 5.7 %copy-start.6 = (bf16[128,1088]{0,1:T(8,128)(2,1)}, bf16[128,1088]{0,1:T(8,128)(2,1)S(1)}, u32[]{:S(2)}) copy-start(bf16[128,1088]{0,1:T(8,128)(2,1)S(1)} %get-tuple-element.62) | copy-start | bytes 835588
  115.1 35.9 %all-gather.13.cloned.1.call-start = ((), (), s32[]{:S(2)}) async-start(), calls=%async_computation.7 | async-start | bytes 1392640 | tf_op jit(solution)/shard_map/all_gather | solution.py:164
  115.7 70.8 %reduce-scatter.20.cloned.1.call-start = ((), (), s32[]{:S(2)}) async-start(), calls=%async_computation.15 | async-start | bytes 1474560
  160.7 79.4 %all-gather.15.cloned.1.call-start = ((), (), s32[]{:S(2)}) async-start(), calls=%async_computation.8 | async-start | bytes 1392640 | tf_op jit(solution)/shard_map/all_gather | solution.py:164
  211.5 10.4 %collective-permute-start.1 = (bf16[128,1088]{0,1:T(8,128)(2,1)}, bf16[128,1088]{0,1:T(8,128)(2,1)}, u32[]{:S(2)}, u32[]{:S(2)}) collective-permute-start(bf16[128,1088]{0,1:T(8,128)(2,1)} %fusion.121), channel_id=1, source_target_pairs={{16,0},{17,1},{18,2},{19,3},{20,4},{21,5},{22,6},{23,7},{24,8},{25... | collective-permute-start | bytes 835592 | tf_op jit(solution)/shard_map/ppermute | solution.py:19
  223.7 49.5 %all-gather.17.cloned.1.call-start = ((), (), s32[]{:S(2)}) async-start(), calls=%async_computation.9 | async-start | bytes 1392640 | tf_op jit(solution)/shard_map/all_gather | solution.py:93
  224.4 80.1 %all-gather.21.cloned.1.call-start = ((), (), s32[]{:S(2)}) async-start(), calls=%async_computation.11 | async-start | bytes 1392640 | tf_op jit(solution)/shard_map/all_gather | solution.py:93
  225.2 106.4 %reduce-scatter.18.cloned.1.call-start = ((), (), s32[]{:S(2)}) async-start(), calls=%async_computation.14 | async-start | bytes 1474560
  232.1 128.2 %reduce-scatter.22.cloned.1.call-start = ((), (), s32[]{:S(2)}) async-start(), calls=%async_computation.16 | async-start | bytes 1474560
  249.8 173.8 %all-gather.19.cloned.1.call-start = ((), (), s32[]{:S(2)}) async-start(), calls=%async_computation.10 | async-start | bytes 5570560 | tf_op jit(solution)/shard_map/all_gather | solution.py:94
  273.2 162.0 %all-gather.23.cloned.1.call-start = ((), (), s32[]{:S(2)}) async-start(), calls=%async_computation.12 | async-start | bytes 5570560 | tf_op jit(solution)/shard_map/all_gather | solution.py:94
  304.5 251.3 %reduce-scatter.24.cloned.1.call-start = ((), (), s32[]{:S(2)}) async-start(), calls=%async_computation.17 | async-start | bytes 10967040
  393.6 8.5 %copy-start.3 = (f32[128,1088]{0,1:T(8,128)S(1)}, f32[128,1088]{0,1:T(8,128)}, u32[]{:S(2)}) copy-start(f32[128,1088]{0,1:T(8,128)} %copy-done.2) | copy-start | bytes 1671172
  435.2 12.6 %copy-start.14 = (bf16[2048,1088]{0,1:T(8,128)(2,1)S(1)}, bf16[2048,1088]{0,1:T(8,128)(2,1)}, u32[]{:S(2)}) copy-start(bf16[2048,1088]{0,1:T(8,128)(2,1)} %all-gather.19.cloned.1.call-done) | copy-start | bytes 13369348
  435.2 20.5 %slice-start = ((s8[8912896]{0:T(1024)(128)(4,1)}), s8[4194304]{0:T(1024)(128)(4,1)S(1)}, s32[]{:S(2)}) async-start(s8[8912896]{0:T(1024)(128)(4,1)} %bitcast.222), calls=%async_computation.18 | async-start | bytes 8388608
  435.2 20.5 %slice-start.1 = ((s8[8912896]{0:T(1024)(128)(4,1)}), s8[4194304]{0:T(1024)(128)(4,1)S(1)}, s32[]{:S(2)}) async-start(s8[8912896]{0:T(1024)(128)(4,1)} %bitcast.222), calls=%async_computation.19 | async-start | bytes 8388608
  447.8 7.9 %copy-start.15 = (bf16[2048,1088]{0,1:T(8,128)(2,1)S(1)}, bf16[2048,1088]{0,1:T(8,128)(2,1)}, u32[]{:S(2)}) copy-start(bf16[2048,1088]{0,1:T(8,128)(2,1)} %all-gather.23.cloned.1.call-done) | copy-start | bytes 13369348
  447.8 7.9 %slice-start.2 = ((s8[8912896]{0:T(1024)(128)(4,1)}), s8[524288]{0:T(1024)(128)(4,1)S(1)}, s32[]{:S(2)}) async-start(s8[8912896]{0:T(1024)(128)(4,1)} %bitcast.222), calls=%async_computation.20 | async-start | bytes 1048576
  (10 other events, 33.0 us)
Sparse Core Ops, SparseCore 0:
  31.0 19.9 all-gather.8
  60.0 25.6 reduce-scatter.15
  115.2 17.1 all-gather.10
  133.8 17.1 all-gather.12
  160.9 25.5 reduce-scatter.19
  223.8 16.2 all-gather.14
  242.2 30.8 all-gather.16
  275.3 29.1 all-gather.20
  307.7 23.8 reduce-scatter.17
  334.6 25.6 reduce-scatter.21
  361.8 35.9 all-gather.18
  399.2 35.9 all-gather.22
  439.3 116.4 reduce-scatter.23

commit v2 on v1

--- a/solution.py
+++ b/solution.py
@@ -1,8 +1,11 @@
+import functools
 import math
 
 import jax
 import jax.numpy as jnp
 from jax import lax
+from jax.experimental import pallas as pl
+from jax.experimental.pallas import tpu as pltpu
 from jax.sharding import PartitionSpec as P
 
 HEADS = 17
@@ -87,6 +90,155 @@
         (((left_dim,), (right_dim,)), ((0,), (0,))),
         preferred_element_type=jnp.float32,
     )
+
+
+def greet(partner, peers):
+    barrier = pltpu.get_barrier_semaphore()
+    for place in [partner] + peers:
+        pl.semaphore_signal(
+            barrier,
+            inc=1,
+            device_id={"tensor": place},
+            device_id_type=pl.DeviceIdType.MESH,
+        )
+    pl.semaphore_wait(barrier, 1 + len(peers))
+
+
+def send(source, target, send_sem, recv_sem, place):
+    copy = pltpu.make_async_remote_copy(
+        src_ref=source,
+        dst_ref=target,
+        send_sem=send_sem,
+        recv_sem=recv_sem,
+        device_id={"tensor": place},
+        device_id_type=pl.DeviceIdType.MESH,
+    )
+    copy.start()
+    return copy
+
+
+def gather_kernel(chips, rows, own_ref, out_ref, send_sem, recv_sem):
+    me = lax.axis_index("tensor")
+    core = lax.rem(me, 2)
+    chip = me // 2
+    partner = me + 1 - 2 * core
+    peers = [lax.rem(chip + k, chips) * 2 + core for k in range(1, chips)]
+    greet(partner, peers)
+
+    def block(index):
+        return out_ref.at[pl.ds(pl.multiple_of(index * rows, rows), rows)]
+
+    across = [
+        send(own_ref, block(me), send_sem.at[k], recv_sem.at[k], peer)
+        for k, peer in enumerate(peers)
+    ]
+    beside = [send(own_ref, block(me), send_sem.at[chips - 1], recv_sem.at[chips - 1], partner)]
+    out_ref[pl.ds(pl.multiple_of(me * rows, rows), rows)] = own_ref[...]
+    for k, copy in enumerate(across):
+        copy.wait_recv()
+        origin = block(lax.rem(chip + chips - 1 - k, chips) * 2 + core)
+        beside.append(send(origin, origin, send_sem.at[chips + k], recv_sem.at[chips + k], partner))
+    for copy in across:
+        copy.wait_send()
+    for copy in beside:
+        copy.wait()
+
+
+def gather_rows(own):
+    chips = lax.axis_size("tensor") // 2
+    rows, width = own.shape
+    return pl.pallas_call(
+        functools.partial(gather_kernel, chips, rows),
+        out_shape=jax.ShapeDtypeStruct((2 * chips * rows, width), own.dtype),
+        in_specs=[pl.BlockSpec(memory_space=pltpu.VMEM)],
+        out_specs=pl.BlockSpec(memory_space=pltpu.VMEM),
+        scratch_shapes=[
+            pltpu.SemaphoreType.DMA((2 * chips - 1,)),
+            pltpu.SemaphoreType.DMA((2 * chips - 1,)),
+        ],
+        compiler_params=pltpu.CompilerParams(collective_id=0, has_side_effects=True),
+    )(own)
+
+
+def scatter_kernel(
+    chips,
+    rows,
+    part_ref,
+    out_ref,
+    beside_buf,
+    stage_buf,
+    across_buf,
+    beside_send,
+    beside_recv,
+    across_send,
+    across_recv,
+):
+    me = lax.axis_index("tensor")
+    core = lax.rem(me, 2)
+    chip = me // 2
+    partner = me + 1 - 2 * core
+    targets = [lax.rem(chip + 1 + k, chips) for k in range(chips)]
+    peers = [target * 2 + core for target in targets[:-1]]
+    greet(partner, peers)
+
+    def span(index):
+        return pl.ds(pl.multiple_of(index * rows, rows), rows)
+
+    beside = [
+        send(
+            part_ref.at[span(target * 2 + 1 - core)],
+            beside_buf.at[k],
+            beside_send.at[k],
+            beside_recv.at[k],
+            partner,
+        )
+        for k, target in enumerate(targets)
+    ]
+    across = []
+    for k, target in enumerate(targets):
+        beside[k].wait_recv()
+        total = part_ref[span(target * 2 + core)].astype(jnp.float32)
+        total = total + beside_buf[k].astype(jnp.float32)
+        if k < chips - 1:
+            stage_buf[k] = total.astype(stage_buf.dtype)
+            across.append(
+                send(
+                    stage_buf.at[k],
+                    across_buf.at[k],
+                    across_send.at[k],
+                    across_recv.at[k],
+                    peers[k],
+                )
+            )
+        else:
+            out_ref[...] = total
+    for k, copy in enumerate(across):
+        copy.wait_recv()
+        out_ref[...] += across_buf[k].astype(jnp.float32)
+    for copy in beside + across:
+        copy.wait_send()
+
+
+def scatter_rows(parts):
+    chips = lax.axis_size("tensor") // 2
+    rows, width = parts.shape[0] // (2 * chips), parts.shape[1]
+    hops = max(chips - 1, 1)
+    return pl.pallas_call(
+        functools.partial(scatter_kernel, chips, rows),
+        out_shape=jax.ShapeDtypeStruct((rows, width), jnp.float32),
+        in_specs=[pl.BlockSpec(memory_space=pltpu.VMEM)],
+        out_specs=pl.BlockSpec(memory_space=pltpu.VMEM),
+        scratch_shapes=[
+            pltpu.VMEM((chips, rows, width), parts.dtype),
+            pltpu.VMEM((hops, rows, width), parts.dtype),
+            pltpu.VMEM((hops, rows, width), parts.dtype),
+            pltpu.SemaphoreType.DMA((chips,)),
+            pltpu.SemaphoreType.DMA((chips,)),
+            pltpu.SemaphoreType.DMA((hops,)),
+            pltpu.SemaphoreType.DMA((hops,)),
+        ],
+        compiler_params=pltpu.CompilerParams(collective_id=1, has_side_effects=True),
+    )(parts)
 
 
 def gather_all(rows):
@@ -115,15 +267,12 @@
     residual = inflow + jnp.dot(mixed, w_out, preferred_element_type=jnp.float32) + biases[3]
     normed_two, inverse_two = norm_rows(residual)
     normal_two = (normed_two * gains[1] + biases[4]).astype(jnp.bfloat16)
-    gathered = lax.all_gather(normal_two, "tensor", axis=0, tiled=True)
+    gathered = gather_rows(normal_two)
     hidden_pre = jnp.dot(gathered, w_up, preferred_element_type=jnp.float32) + up_bias
     hidden = gelu_tanh(hidden_pre).astype(jnp.bfloat16)
-    branch = lax.psum_scatter(
-        jnp.dot(hidden, w_down, preferred_element_type=jnp.float32).astype(jnp.bfloat16),
-        "tensor",
-        scatter_dimension=0,
-        tiled=True,
-    ).astype(jnp.float32)
+    branch = scatter_rows(
+        jnp.dot(hidden, w_down, preferred_element_type=jnp.float32).astype(jnp.bfloat16)
+    )
     result = (residual + branch + biases[5]).astype(jnp.bfloat16)
     kept = (
         normal_one,
@@ -161,16 +310,11 @@
     row_count, model_width = grad_out.shape
     head_width = model_width // HEADS
     grad_flow = grad_out.astype(jnp.float32)
-    grad_rows = lax.all_gather(grad_out, "tensor", axis=0, tiled=True)
+    grad_rows = gather_rows(grad_out)
     grad_hidden = contract_cols(grad_rows, w_down)
     grad_pre = grad_hidden * gelu_slope(hidden_pre)
     grad_pre_b = grad_pre.astype(jnp.bfloat16)
-    grad_two = lax.psum_scatter(
-        contract_cols(grad_pre_b, w_up).astype(jnp.bfloat16),
-        "tensor",
-        scatter_dimension=0,
-        tiled=True,
-    ).astype(jnp.float32)
+    grad_two = scatter_rows(contract_cols(grad_pre_b, w_up).astype(jnp.bfloat16))
     grad_resid = grad_flow + norm_back(grad_two, normed_two, inverse_two, gains[1])
     grad_resid_b = grad_resid.astype(jnp.bfloat16)
     grad_mixed = head_split(contract_cols(grad_resid_b, w_out).astype(jnp.bfloat16))

time: 579 us -> 496 us (0.86)
  waiting for transfers between devices: 313 us -> 118 us
  Pallas kernels: 0 us -> 123 us
  starting transfers between devices: 17 us -> 5.12 us
    pallas_call x0 -> x8, Pallas kernels: none -> 123 us  [the longest x4 65.3 us: scatter_rows(): pl.pallas_call(functools.partial(scatter_kernel, chips, rows), out_shape=...]
    unnamed x18 -> x6, waiting for transfers between devices: 185 us -> 66.2 us
    all_gather x4 -> x0, waiting for transfers between devices: 58.2 us -> none  [the longest x2 36.7 us: layer_forward(): gathered = lax.all_gather(normal_two, 'tensor', axis=0, tiled=True)]
    all_gather x2, waiting for transfers between devices: 54.6 us -> 41.7 us  [gather_all(): over_dp = lax.all_gather(rows, 'dp', axis=0, tiled=True)]
    all_gather x4 -> x0, starting transfers between devices: 11.7 us -> none  [the longest x2 11.6 us: layer_backward(): grad_rows = lax.all_gather(grad_out, 'tensor', axis=0, tiled=True)]
    convert_element_type x0 -> x4, local copies, waits for them, and re-layouts: none -> 9.99 us  [the longest x2 5.11 us: layer_backward(): contract_cols(grad_pre_b, w_up).astype(jnp.bfloat16)]
    unnamed x50 -> x44, local copies, waits for them, and re-layouts: 21.8 us -> 12.5 us
  transfers between devices with their start and end apart: 15 -> 7, of which waited for: 14 -> 4; matrix products, arithmetic and copies ran while one was open for 23% -> 28% of each run, Pallas kernels for 0% -> 14%
where the time goes in v2:
time: 496 us; the launch traced here: 486 us
  matrix products  149 us (30%)
  Pallas kernels  123 us (25%)
  waiting for transfers between devices  118 us (24%)
  local copies, waits for them, and re-layouts  55.2 us (11%)
  other arithmetic  20.6 us (4%)
  between operations  16.2 us (3%)
  starting transfers between devices  5.12 us (1%)
    unnamed x6, waiting for transfers between devices  66.2 us
    pallas_call x4, Pallas kernels, scatter_rows(): pl.pallas_call(functools.partial(scatter_kernel, chips, rows), out_shape=...  65.3 us
    pallas_call x4, Pallas kernels, gather_rows(): pl.pallas_call(functools.partial(gather_kernel, chips, rows), out_shape=j...  57.6 us
    dot_general x7, matrix products, contract_cols(): lax.dot_general(left, right, (((1,), (1,)), ((), ())), preferred_element_...  43.4 us
    all_gather x2, waiting for transfers between devices, gather_all(): over_dp = lax.all_gather(rows, 'dp', axis=0, tiled=True)  41.7 us
    dot_general x11, matrix products, batched(): lax.dot_general(left, right, (((left_dim,), (right_dim,)), ((0,), (0,))),...  29.6 us
    dot_general x4, matrix products, contract_rows(): lax.dot_general(left, right, (((0,), (0,)), ((), ())), preferred_element_...  27.6 us
    concatenate x4, local copies, waits for them, and re-layouts, per_device(): jnp.concatenate([grad_wqkv, grad_wout, small.T], axis=1)  26.2 us
  transfers between devices with their start and end apart: 7, of which 4 were waited for; matrix products, arithmetic and copies ran while one was open for 28% of the time, Pallas kernels for 14%

profile of v2, /device:TPU:0, one launch (start us, length us, event | category | flops | bytes accessed | tf_op | source)
XLA Modules:
  0.0 486.1 jit_solution(10771722389429889541)
XLA Ops:
  11.4 6.1 %fusion.15 = f32[128,3264]{0,1:T(8,128)S(1)} fusion(bf16[1,1088,3264]{2,1,0:T(8,128)(2,1)} %param.12, bf16[128,1088]{1,0:T(8,128)(2,1)S(1)} %copy.140, f32[1088]{0:T(1024)S(1)} %get-tuple-element.69, f32[1088]{0:T(1024)S(1)} %get-tuple-element.72, f32[128]{0:T(128)S(1)} %add_rsqrt_fusion.3, f32[128]{0:T(128)S(1)} %broadcast_multiply_fusion.11), kind=kOutput, calls=%fused_computation.23 | convolution fusion | flops 909950976 | bytes 9061888 | tf_op jit(solution)/shard_map/dot_general | solution.py:256
  30.0 13.9 %shard_map.169 = bf16[512,1088]{1,0:T(8,128)(2,1)} custom-call(bf16[128,1088]{1,0:T(8,128)(2,1)} %add_convert_fusion.3.own_ref), custom_call_target="tpu_custom_call" | custom-call | tf_op jit(solution)/shard_map/pallas_call | solution.py:150
  43.9 6.6 %convolution_convert_fusion.5 = bf16[512,1088]{0,1:T(8,128)(2,1)} fusion(bf16[1,1088,1088]{2,1,0:T(8,128)(2,1)S(1)} %copy-done, bf16[512,1088]{1,0:T(8,128)(2,1)} %shard_map.169, bf16[1,1088,1088]{2,1,0:T(8,128)(2,1)} %param.14, f32[1088]{0:T(1024)S(1)} %reduce.10), kind=kOutput, calls=%fused_computation.43 | convolution fusion | flops 2430435328 | bytes 6967552 | tf_op jit(solution)/shard_map/dot_general | solution.py:274
  52.8 13.0 %shard_map.170 = f32[128,1088]{1,0:T(8,128)} custom-call(bf16[512,1088]{1,0:T(8,128)(2,1)} %copy.139.part_ref), custom_call_target="tpu_custom_call" | custom-call | tf_op jit(solution)/shard_map/pallas_call | solution.py:226
  73.2 12.0 %shard_map.173 = bf16[512,1088]{1,0:T(8,128)(2,1)} custom-call(bf16[128,1088]{1,0:T(8,128)(2,1)} %copy.151.own_ref), custom_call_target="tpu_custom_call" | custom-call | tf_op jit(solution)/shard_map/pallas_call | solution.py:150
  85.6 6.1 %fusion.13 = f32[128,3264]{0,1:T(8,128)S(1)} fusion(bf16[1,1088,3264]{2,1,0:T(8,128)(2,1)} %param.12, bf16[128,1088]{1,0:T(8,128)(2,1)S(1)} %get-tuple-element.78, f32[128]{0:T(128)S(1)} %add_rsqrt_fusion.1, f32[128]{0:T(128)S(1)} %broadcast_multiply_fusion.9, f32[1088]{0:T(1024)S(1)} %get-tuple-element.69, f32[1088]{0:T(1024)S(1)} %get-tuple-element.72), kind=kOutput, calls=%fused_computation.21 | convolution fusion | flops 909950976 | bytes 9061888 | tf_op jit(solution)/shard_map/dot_general | solution.py:256
  101.5 12.6 %shard_map.171 = bf16[512,1088]{1,0:T(8,128)(2,1)} custom-call(bf16[128,1088]{1,0:T(8,128)(2,1)} %add_convert_fusion.1.own_ref), custom_call_target="tpu_custom_call" | custom-call | tf_op jit(solution)/shard_map/pallas_call | solution.py:150
  119.1 7.4 %convolution_convert_fusion.3 = bf16[512,1088]{0,1:T(8,128)(2,1)} fusion(bf16[1,1088,1088]{2,1,0:T(8,128)(2,1)} %param.14, bf16[512,1088]{1,0:T(8,128)(2,1)} %shard_map.173, bf16[1,1088,1088]{2,1,0:T(8,128)(2,1)S(1)} %copy-done, f32[512,1088]{0,1:T(8,128)} %convolution_add_fusion.1), kind=kOutput, calls=%fused_computation.41 | convolution fusion | flops 2435448832 | bytes 9191424 | tf_op jit(solution)/shard_map/dot_general | solution.py:62
  129.3 13.0 %shard_map.174 = f32[128,1088]{1,0:T(8,128)} custom-call(bf16[512,1088]{1,0:T(8,128)(2,1)} %copy.146.part_ref), custom_call_target="tpu_custom_call" | custom-call | tf_op jit(solution)/shard_map/pallas_call | solution.py:226
  167.9 9.7 %collective-permute-done.1 = bf16[128,1088]{1,0:T(8,128)(2,1)} collective-permute-done((bf16[128,1088]{1,0:T(8,128)(2,1)}, bf16[128,1088]{1,0:T(8,128)(2,1)}, u32[]{:S(2)}, u32[]{:S(2)}) %collective-permute-start.1) | collective-permute-done | bytes 278560 | tf_op jit(solution)/shard_map/ppermute | solution.py:22
  179.4 10.1 %all-gather.5.cloned.1.call-done = bf16[512,1088]{1,0:T(8,128)(2,1)} async-done(((bf16[128,1088]{1,0:T(8,128)(2,1)}), bf16[512,1088]{1,0:T(8,128)(2,1)}) %all-gather.5.cloned.1.call-update) | async-done | bytes 1114128 | tf_op jit(solution)/shard_map/all_gather | solution.py:245
  189.6 31.6 %all-gather.9.cloned.1.call-done = bf16[512,1088]{1,0:T(8,128)(2,1)} async-done(((bf16[128,1088]{1,0:T(8,128)(2,1)}), bf16[512,1088]{1,0:T(8,128)(2,1)}) %all-gather.9.cloned.1.call-update) | async-done | bytes 1114128 | tf_op jit(solution)/shard_map/all_gather | solution.py:245
  228.1 19.8 %shard_map.172 = f32[128,1088]{1,0:T(8,128)} custom-call(bf16[512,1088]{1,0:T(8,128)(2,1)} %copy.143.part_ref), custom_call_target="tpu_custom_call" | custom-call | tf_op jit(solution)/shard_map/pallas_call | solution.py:226
  249.7 19.2 %shard_map.175 = bf16[512,1088]{1,0:T(8,128)(2,1)} custom-call(bf16[128,1088]{1,0:T(8,128)(2,1)} %get-tuple-element.74.own_ref), custom_call_target="tpu_custom_call" | custom-call | tf_op jit(solution)/shard_map/pallas_call | solution.py:150
  268.9 7.4 %convolution_convert_fusion.2 = bf16[512,1088]{0,1:T(8,128)(2,1)} fusion(bf16[1,1088,1088]{2,1,0:T(8,128)(2,1)} %param.14, bf16[512,1088]{1,0:T(8,128)(2,1)} %shard_map.175, bf16[1,1088,1088]{2,1,0:T(8,128)(2,1)S(1)} %copy-done, f32[512,1088]{0,1:T(8,128)} %convolution_add_fusion.1), kind=kOutput, calls=%fused_computation.40 | convolution fusion | flops 2435448832 | bytes 9191424 | tf_op jit(solution)/shard_map/dot_general | solution.py:62
  278.6 19.5 %shard_map.176 = f32[128,1088]{1,0:T(8,128)} custom-call(bf16[512,1088]{1,0:T(8,128)(2,1)} %copy.152.part_ref), custom_call_target="tpu_custom_call" | custom-call | tf_op jit(solution)/shard_map/pallas_call | solution.py:226
  320.5 6.3 %convolution_convert_fusion = bf16[1088,3264]{1,0:T(8,128)(2,1)} fusion(bf16[128,1088]{0,1:T(8,128)(2,1)} %bitcast.204, bf16[128,1088]{0,1:T(8,128)(2,1)} %bitcast.200, bf16[128,1088]{0,1:T(8,128)(2,1)} %bitcast.202, bf16[128,1088]{1,0:T(8,128)(2,1)S(1)} %get-tuple-element.78, f32[128]{0:T(128)S(1)} %add_rsqrt_fusion.1, ...), kind=kOutput, calls=%fused_computation.4 | convolution fusion | flops 916008960 | bytes 8226304 | tf_op jit(solution)/shard_map/dot_general | solution.py:56
  326.8 9.2 %concatenate.19 = bf16[16,68,3264]{2,1,0:T(8,128)(2,1)} reshape(bf16[1088,3264]{1,0:T(8,128)(2,1)} %convolution_convert_fusion) | data formatting | bytes 14204928 | tf_op jit(solution)/shard_map/concatenate | solution.py:386
  342.1 15.9 %concatenate.21 = bf16[16,68,4360]{2,1,0:T(8,128)(2,1)} concatenate(bf16[16,68,3264]{2,1,0:T(8,128)(2,1)} %concatenate.19, bf16[16,68,1088]{2,1,0:T(8,128)(2,1)} %convolution_convert_fusion.1, bf16[16,68,8]{2,1,0:T(8,128)(2,1)} %copy.159), dimensions={2} | concatenate | bytes 18974720 | tf_op jit(solution)/shard_map/concatenate | solution.py:386
  363.8 11.6 %convolution_add_fusion = f32[2048,1088]{0,1:T(8,128)} fusion(bf16[2048,1088]{1,0:T(8,128)(2,1)} %all-gather.7.cloned.1.call-done, f32[1088]{0:T(1024)S(1)} %reduce.10, bf16[1,1088,1088]{2,1,0:T(8,128)(2,1)} %param.14), kind=kOutput, calls=%fused_computation.8 | convolution fusion | flops 4850843648 | bytes 15741184 | tf_op jit(solution)/shard_map/dot_general | solution.py:337
  375.4 12.8 %fusion.198 = (f32[1088]{0:T(1024)S(1)}, bf16[2048,1088]{0,1:T(8,128)(2,1)S(1)}) fusion(f32[2048,1088]{0,1:T(8,128)} %convolution_add_fusion, bf16[2048,1088]{1,0:T(8,128)(2,1)} %all-gather.11.cloned.1.call-done, bf16[1,1088,1088]{2,1,0:T(8,128)(2,1)S(1)} %copy-done), kind=kOutput, calls=%fused_computation.269 | convolution fusion | flops 4893178880 | bytes 20197632 | tf_op jit(solution)/shard_map/dot_general | solution.py:62
  388.8 8.7 %convolution_bitcast_fusion.1 = f32[1,1088,1088]{2,1,0:T(8,128)} fusion(bf16[2048,1088]{1,0:T(8,128)(2,1)S(1)} %copy-done.13, bf16[2048,1088]{0,1:T(8,128)(2,1)S(1)} %get-tuple-element.100), kind=kOutput, calls=%fused_computation.16 | convolution fusion | flops 4848615424 | bytes 13647872 | tf_op jit(solution)/shard_map/dot_general | solution.py:56
  397.5 9.2 %convolution_bitcast_fusion = f32[1,1088,1088]{2,1,0:T(8,128)} fusion(bf16[2048,1088]{1,0:T(8,128)(2,1)S(1)} %copy-done.14, f32[2048,1088]{0,1:T(8,128)S(1)} %bitcast.219), kind=kOutput, calls=%fused_computation.15 | convolution fusion | flops 4868669440 | bytes 18104320 | tf_op jit(solution)/shard_map/dot_general | solution.py:56
  406.7 66.1 %reduce-scatter.4.cloned.1.call-done = bf16[1,68,4360]{2,1,0:T(8,128)(2,1)} async-done(((bf16[16,68,4360]{2,1,0:T(8,128)(2,1)}), bf16[1,68,4360]{2,1,0:T(8,128)(2,1)}) %reduce-scatter.4.cloned.1.call-update) | async-done | bytes 592976
  (150 shorter events, 122.2 us)
Async XLA Ops:
  8.0 35.9 %copy-start = (bf16[1,1088,1088]{2,1,0:T(8,128)(2,1)S(1)}, bf16[1,1088,1088]{2,1,0:T(8,128)(2,1)}, u32[]{:S(2)}) copy-start(bf16[1,1088,1088]{2,1,0:T(8,128)(2,1)} %param.16) | copy-start | bytes 7102468
  8.0 181.5 %all-gather.5.cloned.1.call-start = ((), (), s32[]{:S(2)}) async-start(), calls=%async_computation.1 | async-start | bytes 1474560 | tf_op jit(solution)/shard_map/all_gather | solution.py:245
  11.4 7.4 %copy-start.12 = (s32[1,2,4]{2,1,0:T(2,128)S(1)}, s32[1,2,4]{2,1,0:T(2,128)}, u32[]{:S(2)}) copy-start(s32[1,2,4]{2,1,0:T(2,128)} %param.11) | copy-start | bytes 100
  17.6 1.2 copy-start.6
  28.8 15.0 %copy-start.11 = (f32[1,1088]{1,0:T(1,128)S(1)}, f32[1,1088]{1,0:T(1,128)}, u32[]{:S(2)}) copy-start(f32[1,1088]{1,0:T(1,128)} %param.15) | copy-start | bytes 13060
  67.7 17.5 %collective-permute-start = (bf16[128,1088]{1,0:T(8,128)(2,1)}, bf16[128,1088]{1,0:T(8,128)(2,1)S(1)}, u32[]{:S(2)}, u32[]{:S(2)}) collective-permute-start(bf16[128,1088]{1,0:T(8,128)(2,1)} %add_convert_fusion.2), channel_id=1, source_target_pairs={{0,16},{1,17},{2,18},{3,19},{4,20},{5,21},{6,22},{7,23},{8,24},{9,... | collective-permute-start | bytes 835592 | tf_op jit(solution)/shard_map/ppermute | solution.py:22
  92.1 5.7 %copy-start.7 = (bf16[128,1088]{0,1:T(8,128)(2,1)}, bf16[128,1088]{0,1:T(8,128)(2,1)S(1)}, u32[]{:S(2)}) copy-start(bf16[128,1088]{0,1:T(8,128)(2,1)S(1)} %get-tuple-element.80) | copy-start | bytes 835588
  92.1 5.7 %copy-start.9 = (bf16[128,1088]{0,1:T(8,128)(2,1)}, bf16[128,1088]{0,1:T(8,128)(2,1)S(1)}, u32[]{:S(2)}) copy-start(bf16[128,1088]{0,1:T(8,128)(2,1)S(1)} %get-tuple-element.79) | copy-start | bytes 835588
  159.3 61.8 %all-gather.9.cloned.1.call-start = ((), (), s32[]{:S(2)}) async-start(), calls=%async_computation.3 | async-start | bytes 1474560 | tf_op jit(solution)/shard_map/all_gather | solution.py:245
  159.4 6.1 %copy-start.4 = (f32[128,1088]{1,0:T(8,128)S(1)}, f32[128,1088]{1,0:T(8,128)}, u32[]{:S(2)}) copy-start(f32[128,1088]{1,0:T(8,128)} %shard_map.174) | copy-start | bytes 1671172
  159.4 6.1 %copy-start.5 = (bf16[128,1088]{1,0:T(8,128)(2,1)S(1)}, bf16[128,1088]{1,0:T(8,128)(2,1)}, u32[]{:S(2)}) copy-start(bf16[128,1088]{1,0:T(8,128)(2,1)} %copy.151.own_ref) | copy-start | bytes 835588
  166.6 11.0 %collective-permute-start.1 = (bf16[128,1088]{1,0:T(8,128)(2,1)}, bf16[128,1088]{1,0:T(8,128)(2,1)}, u32[]{:S(2)}, u32[]{:S(2)}) collective-permute-start(bf16[128,1088]{1,0:T(8,128)(2,1)} %fusion.118), channel_id=1, source_target_pairs={{16,0},{17,1},{18,2},{19,3},{20,4},{21,5},{22,6},{23,7},{24,8},{25... | collective-permute-start | bytes 835592 | tf_op jit(solution)/shard_map/ppermute | solution.py:22
  179.4 184.4 %all-gather.7.cloned.1.call-start = ((), (), s32[]{:S(2)}) async-start(), calls=%async_computation.2 | async-start | bytes 5898240 | tf_op jit(solution)/shard_map/all_gather | solution.py:246
  189.5 185.9 %all-gather.11.cloned.1.call-start = ((), (), s32[]{:S(2)}) async-start(), calls=%async_computation.4 | async-start | bytes 5898240 | tf_op jit(solution)/shard_map/all_gather | solution.py:246
  221.2 251.6 %reduce-scatter.4.cloned.1.call-start = ((), (), s32[]{:S(2)}) async-start(), calls=%async_computation.5 | async-start | bytes 10967040
  298.1 3.9 copy-start.1
  301.9 1.1 copy-start.8
  302.0 2.5 copy-start.10
  326.8 11.9 %copy-start.3 = (f32[128,1088]{1,0:T(8,128)S(1)}, f32[128,1088]{1,0:T(8,128)}, u32[]{:S(2)}) copy-start(f32[128,1088]{1,0:T(8,128)} %copy-done.2) | copy-start | bytes 1671172
  375.4 13.4 %copy-start.13 = (bf16[2048,1088]{1,0:T(8,128)(2,1)S(1)}, bf16[2048,1088]{1,0:T(8,128)(2,1)}, u32[]{:S(2)}) copy-start(bf16[2048,1088]{1,0:T(8,128)(2,1)} %all-gather.7.cloned.1.call-done) | copy-start | bytes 13369348
  375.4 22.1 %slice-start = ((s8[8912896]{0:T(1024)(128)(4,1)}), s8[4194304]{0:T(1024)(128)(4,1)S(1)}, s32[]{:S(2)}) async-start(s8[8912896]{0:T(1024)(128)(4,1)} %bitcast.218), calls=%async_computation.6 | async-start | bytes 8388608
  375.4 22.1 %slice-start.1 = ((s8[8912896]{0:T(1024)(128)(4,1)}), s8[4194304]{0:T(1024)(128)(4,1)S(1)}, s32[]{:S(2)}) async-start(s8[8912896]{0:T(1024)(128)(4,1)} %bitcast.218), calls=%async_computation.7 | async-start | bytes 8388608
  388.8 8.7 %copy-start.14 = (bf16[2048,1088]{1,0:T(8,128)(2,1)S(1)}, bf16[2048,1088]{1,0:T(8,128)(2,1)}, u32[]{:S(2)}) copy-start(bf16[2048,1088]{1,0:T(8,128)(2,1)} %all-gather.11.cloned.1.call-done) | copy-start | bytes 13369348
  388.8 8.7 %slice-start.2 = ((s8[8912896]{0:T(1024)(128)(4,1)}), s8[524288]{0:T(1024)(128)(4,1)S(1)}, s32[]{:S(2)}) async-start(s8[8912896]{0:T(1024)(128)(4,1)} %bitcast.218), calls=%async_computation.8 | async-start | bytes 1048576
  (1 other events, 0.8 us)
Sparse Core Ops, SparseCore 0:
  159.5 29.9 all-gather.4
  191.6 29.4 all-gather.8
  222.7 49.2 all-gather.6
  273.5 43.7 all-gather.10
Sparse Core Ops, SparseCore 1:
  358.1 114.6 reduce-scatter.3
